TPU v7x, 32 devices: a whole 2x2x4 slice. The times are simulated.
32 devices in a mesh: seq: 8 (over z, y), tensor: 4 (over x, core).
Axes of the slice: x: 2, y: 2, z: 4, core: 2. Of those that a mesh axis runs over, the one named last changes fastest.
Arguments:
- residual: bfloat16 [4608, 6144], P('seq', 'tensor'), may hold values from -4 to 4
- queries: bfloat16 [4608, 4096], P(('seq', 'tensor')), may hold values from -6 to 6
- key_rows: bfloat16 [4608, 4096], P(('seq', 'tensor')), may hold values from -6 to 6
- value_rows: bfloat16 [4608, 4096], P(('seq', 'tensor')), may hold values from -6 to 6
- w_out: bfloat16 [4096, 6144], P(None, 'tensor'), may hold values from -0.09375 to 0.09375
- out_gate: float32 [6144], P('tensor'), may hold values from 0.5 to 1.5
- extents: int32 [32, 3], replicated, may hold values from 0 to 1, as said below
Outputs:
- updated: bfloat16 [4608, 6144], P('seq', 'tensor')
Inputs may be any that keep to these rules, and one draw needn't show every extreme that they name: `extents`: reaches in tile-frames are at most 1, in tile-rows at most 1, in tile-columns at most 1; each of these bounds is taken by some head, and some head has reach 0 in tile-rows.
All inputs are finite; a program needn't handle non-finite values.
Results may differ from a plain program's by a relative error of at most 0.0048.
Values may be sent and summed in bfloat16 or wider, within the bound.
A program may use at most 192 MiB of HBM per device.

v0:
```python
import math
import jax
import jax.numpy as jnp
from jax import lax
from jax.sharding import PartitionSpec as P

HEAD_DIM = 128
TILE = 32
HT_DEV = 2
WT = 3


def passed_along(value, axis, by):
    length = lax.axis_size(axis)
    pairs = [(i, i + by) for i in range(length) if 0 <= i + by < length]
    return lax.ppermute(value, axis, pairs)


def tile_coords(row_count, tile_rows, first_row):
    position = jnp.arange(row_count, dtype=jnp.int32)
    frame_id = position // (tile_rows * WT * TILE)
    row_id = first_row + position // (WT * TILE) % tile_rows
    col_id = position // TILE % WT
    return (frame_id, row_id, col_id)


def allowed_keys(query_place, key_place, head_reach, seq_block, seq_count):
    frame_gap = jnp.abs(query_place[0][:, None] - key_place[0][None, :])
    row_gap = jnp.abs(query_place[1][:, None] - key_place[1][None, :])
    col_gap = jnp.abs(query_place[2][:, None] - key_place[2][None, :])
    global_row = key_place[1] + seq_block * HT_DEV
    inside = (global_row >= 0) & (global_row < seq_count * HT_DEV)
    return (
        (frame_gap[None] <= head_reach[:, 0, None, None])
        & (row_gap[None] <= head_reach[:, 1, None, None])
        & (col_gap[None] <= head_reach[:, 2, None, None])
        & inside[None, None, :]
    )


def shards(residual, queries, key_rows, value_rows, w_out, out_gate, extents):
    head_q, head_k, head_v = (
        lax.all_to_all(queries, "tensor", split_axis=1, concat_axis=0, tiled=True),
        lax.all_to_all(key_rows, "tensor", split_axis=1, concat_axis=0, tiled=True),
        lax.all_to_all(value_rows, "tensor", split_axis=1, concat_axis=0, tiled=True),
    )
    tokens = head_q.shape[0]
    inner_dev = head_q.shape[1]
    head_dim = HEAD_DIM
    heads_here = inner_dev // head_dim
    seq_block = lax.axis_index("seq")
    seq_count = lax.axis_size("seq")
    head_reach = lax.dynamic_slice_in_dim(
        extents, lax.axis_index("tensor") * heads_here, heads_here, 0
    )
    query_tiles = head_q.reshape(tokens, heads_here, head_dim)
    query_place = tile_coords(tokens, HT_DEV, 0)
    stacked = jnp.stack([head_k, head_v])

    def part_scores(pair_rows, key_place):
        key_tiles = pair_rows[0].reshape(-1, heads_here, head_dim)
        scores = jnp.einsum(
            "qhd,khd->hqk", query_tiles, key_tiles, preferred_element_type=jnp.float32
        ) / math.sqrt(head_dim)
        allowed = allowed_keys(query_place, key_place, head_reach, seq_block, seq_count)
        return jnp.where(allowed, scores, -1e30)

    lower_part = passed_along(stacked, "seq", 1)
    upper_part = passed_along(stacked, "seq", -1)
    remote = [
        (lower_part, tile_coords(tokens, HT_DEV, -HT_DEV)),
        (upper_part, tile_coords(tokens, HT_DEV, HT_DEV)),
    ]
    own_scores = part_scores(stacked, query_place)
    scores = jnp.concatenate(
        [own_scores] + [part_scores(pair_rows, key_place) for pair_rows, key_place in remote],
        axis=-1,
    )
    value_all = jnp.concatenate(
        [stacked[1]] + [pair_rows[1] for pair_rows, key_place in remote], axis=0
    )
    row_max = jnp.max(scores, axis=-1, keepdims=True)
    exp_scores = jnp.exp(scores - row_max)
    row_sum = jnp.sum(exp_scores, axis=-1, keepdims=True)
    weights = (exp_scores / row_sum).astype(jnp.bfloat16)
    attended = jnp.einsum(
        "hqk,khd->qhd",
        weights,
        value_all.reshape(-1, heads_here, head_dim),
        preferred_element_type=jnp.float32,
    )
    head_out = attended.reshape(tokens, inner_dev).astype(jnp.bfloat16)
    projected = jnp.dot(
        lax.all_gather(head_out, "tensor", axis=1, tiled=True),
        w_out,
        preferred_element_type=jnp.float32,
    )
    return (residual.astype(jnp.float32) + out_gate * projected).astype(jnp.bfloat16)


def solution(mesh):
    placed = (
        P("seq", "tensor"),
        P(("seq", "tensor"), None),
        P(("seq", "tensor"), None),
        P(("seq", "tensor"), None),
        P(None, "tensor"),
        P("tensor"),
        P(),
    )
    return jax.shard_map(
        shards, mesh=mesh, in_specs=placed, out_specs=P("seq", "tensor"), check_vma=False
    )
```

profile of v0, /device:TPU:0, one launch (start us, length us, event | category | flops | bytes accessed | tf_op | source)
XLA Modules:
  0.0 309.6 jit_solution(9259472700142970301)
XLA Ops:
  6.5 2.5 copy.92
  9.1 4.2 %all-to-all-start.1 = ((bf16[144,4,1024]{2,0,1:T(8,128)(2,1)}), bf16[144,4,1024]{2,0,1:T(8,128)(2,1)S(1)}, u32[]{:S(2)}, u32[]{:S(2)}) async-start(bf16[144,4,1024]{2,0,1:T(8,128)(2,1)} %bitcast.60), calls=%async_computation.1 | async-start | bytes 2359296 | tf_op jit(solution)/shard_map/all_to_all | solution.py:44
  14.4 14.7 %all-to-all-done.1 = bf16[144,4,1024]{2,0,1:T(8,128)(2,1)S(1)} async-done(((bf16[144,4,1024]{2,0,1:T(8,128)(2,1)}), bf16[144,4,1024]{2,0,1:T(8,128)(2,1)S(1)}, u32[]{:S(2)}, u32[]{:S(2)}) %all-to-all-start.1) | async-done | bytes 1179680 | tf_op jit(solution)/shard_map/all_to_all | solution.py:44
  29.1 3.5 %all-to-all-start = ((bf16[144,4,1024]{2,0,1:T(8,128)(2,1)}), bf16[144,4,1024]{2,0,1:T(8,128)(2,1)S(1)}, u32[]{:S(2)}, u32[]{:S(2)}) async-start(bf16[144,4,1024]{2,0,1:T(8,128)(2,1)} %bitcast.59), calls=%async_computation | async-start | bytes 2359296 | tf_op jit(solution)/shard_map/all_to_all | solution.py:45
  33.9 14.7 %all-to-all-done = bf16[144,4,1024]{2,0,1:T(8,128)(2,1)S(1)} async-done(((bf16[144,4,1024]{2,0,1:T(8,128)(2,1)}), bf16[144,4,1024]{2,0,1:T(8,128)(2,1)S(1)}, u32[]{:S(2)}, u32[]{:S(2)}) %all-to-all-start) | async-done | bytes 1179680 | tf_op jit(solution)/shard_map/all_to_all | solution.py:45
  48.5 3.5 %all-to-all-start.2 = ((bf16[144,4,1024]{2,0,1:T(8,128)(2,1)}), bf16[144,4,1024]{2,0,1:T(8,128)(2,1)S(1)}, u32[]{:S(2)}, u32[]{:S(2)}) async-start(bf16[144,4,1024]{2,0,1:T(8,128)(2,1)} %bitcast.61), calls=%async_computation.2 | async-start | bytes 2359296 | tf_op jit(solution)/shard_map/all_to_all | solution.py:43
  52.1 1.6 pad_maximum_fusion
  53.7 1.3 collective-permute-start.1
  55.7 6.2 %collective-permute-start = (bf16[2,576,1024]{2,1,0:T(8,128)(2,1)}, bf16[2,576,1024]{2,1,0:T(8,128)(2,1)}, u32[]{:S(2)}, u32[]{:S(2)}) collective-permute-start(bf16[2,576,1024]{2,1,0:T(8,128)(2,1)} %pad_maximum_fusion), channel_id=1, source_target_pairs={{0,4},{4,8},{8,12},{12,16},{16,20},{20,24},{24,28},{1,5},{5,9},{9,... | collective-permute-start | bytes 7077896 | tf_op jit(solution)/shard_map/ppermute | solution.py:16
  63.1 2.0 subtract_abs_fusion.2
  65.2 2.7 subtract_abs_fusion
  70.8 8.3 %fusion.36 = (f32[8,576]{1,0:T(8,128)S(1)}, f32[8,576,576]{2,1,0:T(8,128)}) fusion(bf16[576,8,128]{2,1,0:T(8,128)(2,1)S(1)} %bitcast.79, bf16[576,8,128]{2,1,0:T(8,128)(2,1)S(1)} %bitcast.74, pred[576]{0:T(1024)(128)(4,1)S(1)} %copy-done.17, s32[8]{0:T(128)S(1)} %copy-done.13, s32[576,576]{1,0:T(8,128)S(1)} %copy-done.2, s32[8]{0:T(128)S(1)} %get-tuple-element.12, ...), kind=kOutput, calls=%fused_computation.83 | convolution fusion | flops 703360512 | bytes 16976544 | tf_op jit(solution)/shard_map/qhd,khd->hqk/dot_general | solution.py:62
  79.1 30.9 %collective-permute-done.1 = bf16[2,576,1024]{2,1,0:T(8,128)(2,1)} collective-permute-done((bf16[2,576,1024]{2,1,0:T(8,128)(2,1)}, bf16[2,576,1024]{2,1,0:T(8,128)(2,1)}, u32[]{:S(2)}, u32[]{:S(2)}) %collective-permute-start.1) | collective-permute-done | bytes 2359328 | tf_op jit(solution)/shard_map/ppermute | solution.py:16
  110.0 2.1 slice_bitcast_fusion.2
  113.0 47.8 %collective-permute-done = bf16[2,576,1024]{2,1,0:T(8,128)(2,1)} collective-permute-done((bf16[2,576,1024]{2,1,0:T(8,128)(2,1)}, bf16[2,576,1024]{2,1,0:T(8,128)(2,1)}, u32[]{:S(2)}, u32[]{:S(2)}) %collective-permute-start) | collective-permute-done | bytes 2359328 | tf_op jit(solution)/shard_map/ppermute | solution.py:16
  160.8 2.1 slice_bitcast_fusion.3
  164.6 8.1 %fusion.35 = (f32[8,576]{1,0:T(8,128)S(1)}, f32[8,576,576]{2,1,0:T(8,128)}) fusion(bf16[576,8,128]{2,1,0:T(8,128)(2,1)S(1)} %bitcast.75, bf16[576,8,128]{2,1,0:T(8,128)(2,1)S(1)} %bitcast.77, pred[576]{0:T(1024)(128)(4,1)S(1)} %copy-done.10, s32[8]{0:T(128)S(1)} %copy-done.13, s32[576,576]{1,0:T(8,128)S(1)} %copy-done.2, s32[8]{0:T(128)S(1)} %copy-done.12, ...), kind=kOutput, calls=%fused_computation.82 | convolution fusion | flops 703360512 | bytes 16976544 | tf_op jit(solution)/shard_map/qhd,khd->hqk/dot_general | solution.py:62
  172.7 8.1 %fusion.37 = (f32[8,576]{1,0:T(8,128)S(1)}, f32[8,576,576]{2,1,0:T(8,128)}) fusion(bf16[576,8,128]{2,1,0:T(8,128)(2,1)S(1)} %bitcast.76, bf16[576,8,128]{2,1,0:T(8,128)(2,1)S(1)} %bitcast.78, pred[576]{0:T(1024)(128)(4,1)S(1)} %copy-done.9, s32[8]{0:T(128)S(1)} %copy-done.13, s32[576,576]{1,0:T(8,128)S(1)} %copy-done.2, s32[8]{0:T(128)S(1)} %copy-done.12, ...), kind=kOutput, calls=%fused_computation.84 | convolution fusion | flops 703360512 | bytes 16976544 | tf_op jit(solution)/shard_map/qhd,khd->hqk/dot_general | solution.py:62
  181.4 36.3 %concatenate.17 = f32[8,576,1728]{2,1,0:T(8,128)} concatenate(f32[8,576,576]{2,1,0:T(8,128)} %get-tuple-element.18, f32[8,576,576]{2,1,0:T(8,128)} %get-tuple-element.20, f32[8,576,576]{2,1,0:T(8,128)} %get-tuple-element.16), dimensions={2} | concatenate | bytes 63700992 | tf_op jit(solution)/shard_map/concatenate | solution.py:75
  217.7 14.1 %fusion = f32[8,576]{1,0:T(8,128)} fusion(f32[8,576,1728]{2,1,0:T(8,128)} %concatenate.17, f32[8,576]{1,0:T(8,128)} %maximum_maximum_fusion), kind=kLoop, calls=%fused_computation.2 | loop fusion | flops 15920640 | bytes 31887360 | tf_op jit(solution)/shard_map/reduce_sum | solution.py:84
  231.8 14.3 %fusion.13 = bf16[8,72,8,128]{3,2,1,0:T(8,128)(2,1)} fusion(bf16[576,8,128]{2,0,1:T(8,128)(2,1)S(1)} %copy.41, bf16[576,8,128]{2,0,1:T(8,128)(2,1)S(1)} %copy.40, bf16[576,8,128]{2,0,1:T(8,128)(2,1)S(1)} %copy.39, f32[8,576,1728]{2,1,0:T(8,128)} %concatenate.17, f32[8,576]{1,0:T(8,128)} %fusion, f32[8,576]{1,0:T(8,128)} %maximum_maximum_fusion), kind=kOutput, calls=%fused_computation.30 | convolution fusion | flops 2073526272 | bytes 36605952 | tf_op jit(solution)/shard_map/hqk,khd->qhd/dot_general | solution.py:86
  246.1 2.8 copy.90
  248.9 41.1 %all-gather.2.cloned.1.call-done = bf16[576,4096]{1,0:T(8,128)(2,1)} async-done(((bf16[576,1024]{1,0:T(8,128)(2,1)}), bf16[576,4096]{1,0:T(8,128)(2,1)}) %all-gather.2.cloned.1.call-update) | async-done | bytes 4718608 | tf_op jit(solution)/shard_map/all_gather | solution.py:94
  290.0 12.7 %add_convert_fusion = bf16[576,1536]{1,0:T(8,128)(2,1)} fusion(bf16[576,1536]{1,0:T(8,128)(2,1)S(1)} %copy-done.15, bf16[576,4096]{1,0:T(8,128)(2,1)} %all-gather.2.cloned.1.call-done, bf16[4096,1536]{1,0:T(8,128)(2,1)} %param.11, f32[1536]{0:T(1024)S(1)} %copy-done.16), kind=kOutput, calls=%fused_computation.22 | convolution fusion | flops 7251296256 | bytes 20846592 | tf_op jit(solution)/shard_map/dot_general | solution.py:93
  (60 shorter events, 10.1 us)
Async XLA Ops:
  6.5 55.4 %copy-start = (s32[32,3]{0,1:T(4,128)S(1)}, s32[32,3]{0,1:T(4,128)}, u32[]{:S(2)}) copy-start(s32[32,3]{0,1:T(4,128)} %param.13) | copy-start | bytes 1156
  6.5 6.7 %copy-start.7 = (bf16[144,4096]{1,0:T(8,128)(2,1)S(1)}, bf16[144,4096]{1,0:T(8,128)(2,1)}, u32[]{:S(2)}) copy-start(bf16[144,4096]{1,0:T(8,128)(2,1)} %param.10) | copy-start | bytes 3538948
  9.1 20.1 %all-to-all-start.1 = ((bf16[144,4,1024]{2,0,1:T(8,128)(2,1)}), bf16[144,4,1024]{2,0,1:T(8,128)(2,1)S(1)}, u32[]{:S(2)}, u32[]{:S(2)}) async-start(bf16[144,4,1024]{2,0,1:T(8,128)(2,1)} %bitcast.60), calls=%async_computation.1 | async-start | bytes 2359296 | tf_op jit(solution)/shard_map/all_to_all | solution.py:44
  13.3 19.4 %copy-start.8 = (bf16[144,4096]{1,0:T(8,128)(2,1)S(1)}, bf16[144,4096]{1,0:T(8,128)(2,1)}, u32[]{:S(2)}) copy-start(bf16[144,4096]{1,0:T(8,128)(2,1)} %param.8) | copy-start | bytes 3538948
  29.1 19.4 %all-to-all-start = ((bf16[144,4,1024]{2,0,1:T(8,128)(2,1)}), bf16[144,4,1024]{2,0,1:T(8,128)(2,1)S(1)}, u32[]{:S(2)}, u32[]{:S(2)}) async-start(bf16[144,4,1024]{2,0,1:T(8,128)(2,1)} %bitcast.59), calls=%async_computation | async-start | bytes 2359296 | tf_op jit(solution)/shard_map/all_to_all | solution.py:45
  48.5 19.4 %all-to-all-start.2 = ((bf16[144,4,1024]{2,0,1:T(8,128)(2,1)}), bf16[144,4,1024]{2,0,1:T(8,128)(2,1)S(1)}, u32[]{:S(2)}, u32[]{:S(2)}) async-start(bf16[144,4,1024]{2,0,1:T(8,128)(2,1)} %bitcast.61), calls=%async_computation.2 | async-start | bytes 2359296 | tf_op jit(solution)/shard_map/all_to_all | solution.py:43
  52.0 237.9 %all-gather.2.cloned.1.call-start = ((), (), s32[]{:S(2)}) async-start(), calls=%async_computation.3 | async-start | bytes 5898240 | tf_op jit(solution)/shard_map/all_gather | solution.py:94
  53.7 56.3 %collective-permute-start.1 = (bf16[2,576,1024]{2,1,0:T(8,128)(2,1)}, bf16[2,576,1024]{2,1,0:T(8,128)(2,1)}, u32[]{:S(2)}, u32[]{:S(2)}) collective-permute-start(bf16[2,576,1024]{2,1,0:T(8,128)(2,1)} %pad_maximum_fusion), channel_id=1, source_target_pairs={{4,0},{8,4},{12,8},{16,12},{20,16},{24,20},{28,24},{5,1},{9,5},{13... | collective-permute-start | bytes 7077896 | tf_op jit(solution)/shard_map/ppermute | solution.py:16
  55.7 105.1 %collective-permute-start = (bf16[2,576,1024]{2,1,0:T(8,128)(2,1)}, bf16[2,576,1024]{2,1,0:T(8,128)(2,1)}, u32[]{:S(2)}, u32[]{:S(2)}) collective-permute-start(bf16[2,576,1024]{2,1,0:T(8,128)(2,1)} %pad_maximum_fusion), channel_id=1, source_target_pairs={{0,4},{4,8},{8,12},{12,16},{16,20},{20,24},{24,28},{1,5},{5,9},{9,... | collective-permute-start | bytes 7077896 | tf_op jit(solution)/shard_map/ppermute | solution.py:16
  63.1 6.0 %copy-start.11 = (s32[8]{0:T(128)}, s32[8]{0:T(128)S(1)}, u32[]{:S(2)}) copy-start(s32[8]{0:T(128)S(1)} %get-tuple-element.12) | copy-start | bytes 100
  68.5 1.4 copy-start.2
  68.6 1.8 copy-start.3
  68.6 2.2 copy-start.6
  68.6 2.2 copy-start.13
  68.6 2.2 copy-start.14
  68.6 2.2 copy-start.17
  163.2 1.4 copy-start.5
  163.2 1.4 copy-start.10
  163.2 1.4 copy-start.12
  164.6 8.1 %copy-start.4 = (s32[576,576]{1,0:T(8,128)S(1)}, s32[576,576]{1,0:T(8,128)}, u32[]{:S(2)}) copy-start(s32[576,576]{1,0:T(8,128)} %get-tuple-element.11) | copy-start | bytes 3981316
  164.6 8.1 %copy-start.9 = (pred[576]{0:T(1024)(128)(4,1)S(1)}, pred[576]{0:T(1024)(128)(4,1)}, u32[]{:S(2)}) copy-start(pred[576]{0:T(1024)(128)(4,1)} %get-tuple-element.22) | copy-start | bytes 1732
  246.1 43.9 %copy-start.15 = (bf16[576,1536]{1,0:T(8,128)(2,1)S(1)}, bf16[576,1536]{1,0:T(8,128)(2,1)}, u32[]{:S(2)}) copy-start(bf16[576,1536]{1,0:T(8,128)(2,1)} %param.7) | copy-start | bytes 5308420
  246.1 43.9 %copy-start.16 = (f32[1536]{0:T(1024)S(1)}, f32[1536]{0:T(1024)}, u32[]{:S(2)}) copy-start(f32[1536]{0:T(1024)} %param.12) | copy-start | bytes 18436
  290.0 12.7 %copy-start.1 = (s32[32,3]{0,1:T(4,128)S(1)}, s32[32,3]{0,1:T(4,128)}, u32[]{:S(2)}) copy-start(s32[32,3]{0,1:T(4,128)} %param.13) | copy-start | bytes 1156
Sparse Core Ops, SparseCore 0:
  249.0 40.9 all-gather.1
where the time goes:
time: 311 us; the launch traced here: 310 us
  waiting for transfers between devices  149 us (48%)
  local copies, waits for them, and re-layouts  54.1 us (17%)
  matrix products  51.5 us (17%)
  other arithmetic  22.3 us (7%)
  starting transfers between devices  18.8 us (6%)
  between operations  13.6 us (4%)
    ppermute x2, waiting for transfers between devices, passed_along(): return lax.ppermute(value, axis, pairs)  78.7 us
    all_gather x1, waiting for transfers between devices, shards(): lax.all_gather(head_out, 'tensor', axis=1, tiled=True)  41.1 us
    concatenate x1, local copies, waits for them, and re-layouts, shards(): jnp.concatenate([own_scores] + [part_scores(pair_rows, key_place) for pai...  36.3 us
    dot_general x3, matrix products, part_scores(): jnp.einsum('qhd,khd->hqk', query_tiles, key_tiles, preferred_element_type...  24.5 us
    all_to_all x1, waiting for transfers between devices, shards(): lax.all_to_all(key_rows, 'tensor', split_axis=1, concat_axis=0, tiled=True)  14.7 us
    all_to_all x1, waiting for transfers between devices, shards(): lax.all_to_all(value_rows, 'tensor', split_axis=1, concat_axis=0, tiled=T...  14.7 us
    dot_general x1, matrix products, shards(): jnp.einsum('hqk,khd->qhd', weights, value_all.reshape(-1, heads_here, hea...  14.3 us
    reduce_sum x1, other arithmetic, shards(): row_sum = jnp.sum(exp_scores, axis=-1, keepdims=True)  14.1 us
  transfers between devices with their start and end apart: 6, of which 5 were waited for; matrix products, arithmetic and copies ran while one was open for 7% of the time, Pallas kernels for 0%

commit v1 on v0

--- a/solution.py
+++ b/solution.py
@@ -8,6 +8,27 @@
 TILE = 32
 HT_DEV = 2
 WT = 3
+
+
+def ring_gather(value, axis, dim):
+    count, place, extent = (lax.axis_size(axis), lax.axis_index(axis), value.shape[dim])
+    upward = [(i, (i + 1) % count) for i in range(count)]
+    left = [(i, (i - 1) % count) for i in range(count)]
+    out = jnp.zeros((*value.shape[:dim], count * extent, *value.shape[dim + 1 :]), value.dtype)
+    out = lax.dynamic_update_slice_in_dim(out, value, place * extent, axis=dim)
+    from_left = from_right = value
+    half = count // 2
+    for step in range(1, half + 1):
+        from_left = lax.ppermute(from_left, axis, upward)
+        out = lax.dynamic_update_slice_in_dim(
+            out, from_left, (place - step) % count * extent, axis=dim
+        )
+        if step < count - half:
+            from_right = lax.ppermute(from_right, axis, left)
+            out = lax.dynamic_update_slice_in_dim(
+                out, from_right, (place + step) % count * extent, axis=dim
+            )
+    return out
 
 
 def passed_along(value, axis, by):
@@ -91,9 +112,7 @@
     )
     head_out = attended.reshape(tokens, inner_dev).astype(jnp.bfloat16)
     projected = jnp.dot(
-        lax.all_gather(head_out, "tensor", axis=1, tiled=True),
-        w_out,
-        preferred_element_type=jnp.float32,
+        ring_gather(head_out, "tensor", 1), w_out, preferred_element_type=jnp.float32
     )
     return (residual.astype(jnp.float32) + out_gate * projected).astype(jnp.bfloat16)
 

time: 311 us -> 299 us (0.961)
  between operations: 13.6 us -> 0.34 us
    all_gather x1 -> x0, waiting for transfers between devices: 41.1 us -> none  [shards(): lax.all_gather(head_out, 'tensor', axis=1, tiled=True)]
    ppermute x0 -> x3, waiting for transfers between devices: none -> 37 us  [the longest x2 36.9 us: ring_gather(): from_left = lax.ppermute(from_left, axis, upward)]
    unnamed x45 -> x47, local copies, waits for them, and re-layouts: 9.07 us -> 8.81 us
  transfers between devices with their start and end apart: 6 -> 8, of which waited for: 5 -> 6; matrix products, arithmetic and copies ran while one was open for 7% -> 8% of each run, Pallas kernels for 0% -> 0%
where the time goes in v1:
time: 299 us; the launch traced here: 294 us
  waiting for transfers between devices  146 us (49%)
  local copies, waits for them, and re-layouts  56.1 us (19%)
  matrix products  49.4 us (17%)
  other arithmetic  21.7 us (7%)
  starting transfers between devices  21.4 us (7%)
    ppermute x2, waiting for transfers between devices, passed_along(): return lax.ppermute(value, axis, pairs)  79.2 us
    ppermute x2, waiting for transfers between devices, ring_gather(): from_left = lax.ppermute(from_left, axis, upward)  36.9 us
    concatenate x1, local copies, waits for them, and re-layouts, shards(): jnp.concatenate([own_scores] + [part_scores(pair_rows, key_place) for pai...  36.4 us
    dot_general x3, matrix products, part_scores(): jnp.einsum('qhd,khd->hqk', query_tiles, key_tiles, preferred_element_type...  24.4 us
    all_to_all x1, waiting for transfers between devices, shards(): lax.all_to_all(key_rows, 'tensor', split_axis=1, concat_axis=0, tiled=True)  14.7 us
    all_to_all x1, waiting for transfers between devices, shards(): lax.all_to_all(value_rows, 'tensor', split_axis=1, concat_axis=0, tiled=T...  14.7 us
    reduce_sum x1, other arithmetic, shards(): row_sum = jnp.sum(exp_scores, axis=-1, keepdims=True)  14.1 us
    dot_general x1, matrix products, shards(): jnp.einsum('hqk,khd->qhd', weights, value_all.reshape(-1, heads_here, hea...  13.5 us
  transfers between devices with their start and end apart: 8, of which 6 were waited for; matrix products, arithmetic and copies ran while one was open for 8% of the time, Pallas kernels for 0%

profile of v1, /device:TPU:0, one launch (start us, length us, event | category | flops | bytes accessed | tf_op | source)
XLA Modules:
  0.0 294.5 jit_solution(1346079492995851964)
XLA Ops:
  0.0 2.5 copy.94
  2.5 4.2 %all-to-all-start.1 = ((bf16[144,4,1024]{2,0,1:T(8,128)(2,1)}), bf16[144,4,1024]{2,0,1:T(8,128)(2,1)S(1)}, u32[]{:S(2)}, u32[]{:S(2)}) async-start(bf16[144,4,1024]{2,0,1:T(8,128)(2,1)} %bitcast.62), calls=%async_computation.1 | async-start | bytes 2359296 | tf_op jit(solution)/shard_map/all_to_all | solution.py:65
  7.9 14.7 %all-to-all-done.1 = bf16[144,4,1024]{2,0,1:T(8,128)(2,1)S(1)} async-done(((bf16[144,4,1024]{2,0,1:T(8,128)(2,1)}), bf16[144,4,1024]{2,0,1:T(8,128)(2,1)S(1)}, u32[]{:S(2)}, u32[]{:S(2)}) %all-to-all-start.1) | async-done | bytes 1179680 | tf_op jit(solution)/shard_map/all_to_all | solution.py:65
  22.6 3.5 %all-to-all-start = ((bf16[144,4,1024]{2,0,1:T(8,128)(2,1)}), bf16[144,4,1024]{2,0,1:T(8,128)(2,1)S(1)}, u32[]{:S(2)}, u32[]{:S(2)}) async-start(bf16[144,4,1024]{2,0,1:T(8,128)(2,1)} %bitcast.61), calls=%async_computation | async-start | bytes 2359296 | tf_op jit(solution)/shard_map/all_to_all | solution.py:66
  27.3 14.7 %all-to-all-done = bf16[144,4,1024]{2,0,1:T(8,128)(2,1)S(1)} async-done(((bf16[144,4,1024]{2,0,1:T(8,128)(2,1)}), bf16[144,4,1024]{2,0,1:T(8,128)(2,1)S(1)}, u32[]{:S(2)}, u32[]{:S(2)}) %all-to-all-start) | async-done | bytes 1179680 | tf_op jit(solution)/shard_map/all_to_all | solution.py:66
  42.0 3.5 %all-to-all-start.2 = ((bf16[144,4,1024]{2,0,1:T(8,128)(2,1)}), bf16[144,4,1024]{2,0,1:T(8,128)(2,1)S(1)}, u32[]{:S(2)}, u32[]{:S(2)}) async-start(bf16[144,4,1024]{2,0,1:T(8,128)(2,1)} %bitcast.63), calls=%async_computation.2 | async-start | bytes 2359296 | tf_op jit(solution)/shard_map/all_to_all | solution.py:64
  45.5 1.6 pad_maximum_fusion
  49.1 6.2 %collective-permute-start = (bf16[2,576,1024]{2,1,0:T(8,128)(2,1)}, bf16[2,576,1024]{2,1,0:T(8,128)(2,1)}, u32[]{:S(2)}, u32[]{:S(2)}) collective-permute-start(bf16[2,576,1024]{2,1,0:T(8,128)(2,1)} %pad_maximum_fusion), channel_id=1, source_target_pairs={{0,4},{4,8},{8,12},{12,16},{16,20},{20,24},{24,28},{1,5},{5,9},{9,... | collective-permute-start | bytes 7077896 | tf_op jit(solution)/shard_map/ppermute | solution.py:37
  56.6 2.0 subtract_abs_fusion.2
  58.6 2.7 subtract_abs_fusion
  64.3 8.3 %fusion.36 = (f32[8,576]{1,0:T(8,128)S(1)}, f32[8,576,576]{2,1,0:T(8,128)}) fusion(bf16[576,8,128]{2,1,0:T(8,128)(2,1)S(1)} %bitcast.80, bf16[576,8,128]{2,1,0:T(8,128)(2,1)S(1)} %bitcast.75, pred[576]{0:T(1024)(128)(4,1)S(1)} %copy-done.18, s32[8]{0:T(128)S(1)} %copy-done.14, s32[576,576]{1,0:T(8,128)S(1)} %copy-done.2, s32[8]{0:T(128)S(1)} %get-tuple-element.12, ...), kind=kOutput, calls=%fused_computation.87 | convolution fusion | flops 703360512 | bytes 16976544 | tf_op jit(solution)/shard_map/qhd,khd->hqk/dot_general | solution.py:83
  72.6 30.9 %collective-permute-done.1 = bf16[2,576,1024]{2,1,0:T(8,128)(2,1)} collective-permute-done((bf16[2,576,1024]{2,1,0:T(8,128)(2,1)}, bf16[2,576,1024]{2,1,0:T(8,128)(2,1)}, u32[]{:S(2)}, u32[]{:S(2)}) %collective-permute-start.1) | collective-permute-done | bytes 2359328 | tf_op jit(solution)/shard_map/ppermute | solution.py:37
  103.5 2.1 slice_bitcast_fusion.2
  105.9 48.3 %collective-permute-done = bf16[2,576,1024]{2,1,0:T(8,128)(2,1)} collective-permute-done((bf16[2,576,1024]{2,1,0:T(8,128)(2,1)}, bf16[2,576,1024]{2,1,0:T(8,128)(2,1)}, u32[]{:S(2)}, u32[]{:S(2)}) %collective-permute-start) | collective-permute-done | bytes 2359328 | tf_op jit(solution)/shard_map/ppermute | solution.py:37
  154.2 2.1 slice_bitcast_fusion.3
  158.7 8.1 %fusion.35 = (f32[8,576]{1,0:T(8,128)S(1)}, f32[8,576,576]{2,1,0:T(8,128)}) fusion(bf16[576,8,128]{2,1,0:T(8,128)(2,1)S(1)} %bitcast.76, bf16[576,8,128]{2,1,0:T(8,128)(2,1)S(1)} %bitcast.79, pred[576]{0:T(1024)(128)(4,1)S(1)} %copy-done.11, s32[8]{0:T(128)S(1)} %copy-done.14, s32[576,576]{1,0:T(8,128)S(1)} %copy-done.2, s32[8]{0:T(128)S(1)} %copy-done.13, ...), kind=kOutput, calls=%fused_computation.86 | convolution fusion | flops 703360512 | bytes 16976544 | tf_op jit(solution)/shard_map/qhd,khd->hqk/dot_general | solution.py:83
  166.8 8.1 %fusion.37 = (f32[8,576]{1,0:T(8,128)S(1)}, f32[8,576,576]{2,1,0:T(8,128)}) fusion(bf16[576,8,128]{2,1,0:T(8,128)(2,1)S(1)} %bitcast.77, bf16[576,8,128]{2,1,0:T(8,128)(2,1)S(1)} %bitcast.78, pred[576]{0:T(1024)(128)(4,1)S(1)} %copy-done.10, s32[8]{0:T(128)S(1)} %copy-done.14, s32[576,576]{1,0:T(8,128)S(1)} %copy-done.2, s32[8]{0:T(128)S(1)} %copy-done.13, ...), kind=kOutput, calls=%fused_computation.88 | convolution fusion | flops 703360512 | bytes 16976544 | tf_op jit(solution)/shard_map/qhd,khd->hqk/dot_general | solution.py:83
  174.9 36.4 %concatenate.17 = f32[8,576,1728]{2,1,0:T(8,128)} concatenate(f32[8,576,576]{2,1,0:T(8,128)} %get-tuple-element.18, f32[8,576,576]{2,1,0:T(8,128)} %get-tuple-element.20, f32[8,576,576]{2,1,0:T(8,128)} %get-tuple-element.16), dimensions={2} | concatenate | bytes 63700992 | tf_op jit(solution)/shard_map/concatenate | solution.py:96
  211.8 14.1 %fusion = f32[8,576]{1,0:T(8,128)} fusion(f32[8,576,1728]{2,1,0:T(8,128)} %concatenate.17, f32[8,576]{1,0:T(8,128)S(1)} %maximum_maximum_fusion), kind=kLoop, calls=%fused_computation.2 | loop fusion | flops 15920640 | bytes 31887360 | tf_op jit(solution)/shard_map/reduce_sum | solution.py:105
  225.9 13.5 %fusion.13 = bf16[8,72,8,128]{3,2,1,0:T(8,128)(2,1)S(1)} fusion(bf16[576,8,128]{2,0,1:T(8,128)(2,1)} %copy.41, bf16[576,8,128]{2,0,1:T(8,128)(2,1)S(1)} %copy.40, bf16[576,8,128]{2,0,1:T(8,128)(2,1)S(1)} %copy.39, f32[8,576,1728]{2,1,0:T(8,128)} %concatenate.17, f32[8,576]{1,0:T(8,128)} %fusion, f32[8,576]{1,0:T(8,128)} %copy-done.9), kind=kOutput, calls=%fused_computation.30 | convolution fusion | flops 2073526272 | bytes 36605952 | tf_op jit(solution)/shard_map/hqk,khd->qhd/dot_general | solution.py:107
  240.8 1.7 collective-permute-start.3
  242.5 24.7 %collective-permute-done.2 = bf16[576,1024]{1,0:T(8,128)(2,1)S(1)} collective-permute-done((bf16[576,1024]{1,0:T(8,128)(2,1)}, bf16[576,1024]{1,0:T(8,128)(2,1)S(1)}, u32[]{:S(2)}, u32[]{:S(2)}) %collective-permute-start.2) | collective-permute-done | bytes 1179680 | tf_op jit(solution)/shard_map/ppermute | solution.py:22
  270.6 12.2 %collective-permute-done.4 = bf16[576,1024]{1,0:T(8,128)(2,1)S(1)} collective-permute-done((bf16[576,1024]{1,0:T(8,128)(2,1)S(1)}, bf16[576,1024]{1,0:T(8,128)(2,1)S(1)}, u32[]{:S(2)}, u32[]{:S(2)}) %collective-permute-start.4) | collective-permute-done | bytes 1179680 | tf_op jit(solution)/shard_map/ppermute | solution.py:22
  283.0 11.5 %add_convert_fusion = bf16[576,1536]{1,0:T(8,128)(2,1)} fusion(bf16[576,1536]{1,0:T(8,128)(2,1)S(1)} %copy-done.16, bf16[576,4096]{1,0:T(8,128)(2,1)S(1)} %constant_dynamic-update-slice_fusion, bf16[4096,1536]{1,0:T(8,128)(2,1)} %param.11, f32[1536]{0:T(1024)S(1)} %copy-done.17), kind=kOutput, calls=%fused_computation.22 | convolution fusion | flops 7251296256 | bytes 20846592 | tf_op jit(solution)/shard_map/dot_general | solution.py:114
  (70 shorter events, 16.4 us)
Async XLA Ops:
  0.0 55.3 %copy-start = (s32[32,3]{0,1:T(4,128)S(1)}, s32[32,3]{0,1:T(4,128)}, u32[]{:S(2)}) copy-start(s32[32,3]{0,1:T(4,128)} %param.13) | copy-start | bytes 1156
  0.0 6.7 %copy-start.7 = (bf16[144,4096]{1,0:T(8,128)(2,1)S(1)}, bf16[144,4096]{1,0:T(8,128)(2,1)}, u32[]{:S(2)}) copy-start(bf16[144,4096]{1,0:T(8,128)(2,1)} %param.10) | copy-start | bytes 3538948
  2.5 20.1 %all-to-all-start.1 = ((bf16[144,4,1024]{2,0,1:T(8,128)(2,1)}), bf16[144,4,1024]{2,0,1:T(8,128)(2,1)S(1)}, u32[]{:S(2)}, u32[]{:S(2)}) async-start(bf16[144,4,1024]{2,0,1:T(8,128)(2,1)} %bitcast.62), calls=%async_computation.1 | async-start | bytes 2359296 | tf_op jit(solution)/shard_map/all_to_all | solution.py:65
  6.7 19.4 %copy-start.8 = (bf16[144,4096]{1,0:T(8,128)(2,1)S(1)}, bf16[144,4096]{1,0:T(8,128)(2,1)}, u32[]{:S(2)}) copy-start(bf16[144,4096]{1,0:T(8,128)(2,1)} %param.8) | copy-start | bytes 3538948
  22.6 19.4 %all-to-all-start = ((bf16[144,4,1024]{2,0,1:T(8,128)(2,1)}), bf16[144,4,1024]{2,0,1:T(8,128)(2,1)S(1)}, u32[]{:S(2)}, u32[]{:S(2)}) async-start(bf16[144,4,1024]{2,0,1:T(8,128)(2,1)} %bitcast.61), calls=%async_computation | async-start | bytes 2359296 | tf_op jit(solution)/shard_map/all_to_all | solution.py:66
  42.0 19.4 %all-to-all-start.2 = ((bf16[144,4,1024]{2,0,1:T(8,128)(2,1)}), bf16[144,4,1024]{2,0,1:T(8,128)(2,1)S(1)}, u32[]{:S(2)}, u32[]{:S(2)}) async-start(bf16[144,4,1024]{2,0,1:T(8,128)(2,1)} %bitcast.63), calls=%async_computation.2 | async-start | bytes 2359296 | tf_op jit(solution)/shard_map/all_to_all | solution.py:64
  47.1 56.3 %collective-permute-start.1 = (bf16[2,576,1024]{2,1,0:T(8,128)(2,1)}, bf16[2,576,1024]{2,1,0:T(8,128)(2,1)}, u32[]{:S(2)}, u32[]{:S(2)}) collective-permute-start(bf16[2,576,1024]{2,1,0:T(8,128)(2,1)} %pad_maximum_fusion), channel_id=1, source_target_pairs={{4,0},{8,4},{12,8},{16,12},{20,16},{24,20},{28,24},{5,1},{9,5},{13... | collective-permute-start | bytes 7077896 | tf_op jit(solution)/shard_map/ppermute | solution.py:37
  49.1 105.1 %collective-permute-start = (bf16[2,576,1024]{2,1,0:T(8,128)(2,1)}, bf16[2,576,1024]{2,1,0:T(8,128)(2,1)}, u32[]{:S(2)}, u32[]{:S(2)}) collective-permute-start(bf16[2,576,1024]{2,1,0:T(8,128)(2,1)} %pad_maximum_fusion), channel_id=1, source_target_pairs={{0,4},{4,8},{8,12},{12,16},{16,20},{20,24},{24,28},{1,5},{5,9},{9,... | collective-permute-start | bytes 7077896 | tf_op jit(solution)/shard_map/ppermute | solution.py:37
  56.6 6.0 %copy-start.12 = (s32[8]{0:T(128)}, s32[8]{0:T(128)S(1)}, u32[]{:S(2)}) copy-start(s32[8]{0:T(128)S(1)} %get-tuple-element.12) | copy-start | bytes 100
  62.0 1.8 copy-start.3
  62.0 2.2 copy-start.6
  62.0 2.2 copy-start.14
  62.0 2.2 copy-start.15
  62.0 2.2 copy-start.18
  157.1 1.6 copy-start.5
  157.1 1.6 copy-start.11
  158.7 8.1 %copy-start.4 = (s32[576,576]{1,0:T(8,128)S(1)}, s32[576,576]{1,0:T(8,128)}, u32[]{:S(2)}) copy-start(s32[576,576]{1,0:T(8,128)} %get-tuple-element.11) | copy-start | bytes 3981316
  158.7 8.1 %copy-start.10 = (pred[576]{0:T(1024)(128)(4,1)S(1)}, pred[576]{0:T(1024)(128)(4,1)}, u32[]{:S(2)}) copy-start(pred[576]{0:T(1024)(128)(4,1)} %get-tuple-element.22) | copy-start | bytes 1732
  240.8 26.4 %collective-permute-start.2 = (bf16[576,1024]{1,0:T(8,128)(2,1)}, bf16[576,1024]{1,0:T(8,128)(2,1)S(1)}, u32[]{:S(2)}, u32[]{:S(2)}) collective-permute-start(bf16[576,1024]{1,0:T(8,128)(2,1)} %bitcast.60), channel_id=1, source_target_pairs={{0,1},{1,2},{2,3},{3,0},{4,5},{5,6},{6,7},{7,4},{8,9},{9,10},{10,1... | collective-permute-start | bytes 3538952 | tf_op jit(solution)/shard_map/ppermute | solution.py:22
  240.8 28.2 %collective-permute-start.3 = (bf16[576,1024]{1,0:T(8,128)(2,1)}, bf16[576,1024]{1,0:T(8,128)(2,1)}, u32[]{:S(2)}, u32[]{:S(2)}) collective-permute-start(bf16[576,1024]{1,0:T(8,128)(2,1)} %bitcast.60), channel_id=1, source_target_pairs={{0,3},{1,0},{2,1},{3,2},{4,7},{5,4},{6,5},{7,6},{8,11},{9,8},{10,9... | collective-permute-start | bytes 3538952 | tf_op jit(solution)/shard_map/ppermute | solution.py:27
  267.2 15.6 %collective-permute-start.4 = (bf16[576,1024]{1,0:T(8,128)(2,1)S(1)}, bf16[576,1024]{1,0:T(8,128)(2,1)S(1)}, u32[]{:S(2)}, u32[]{:S(2)}) collective-permute-start(bf16[576,1024]{1,0:T(8,128)(2,1)S(1)} %collective-permute-done.2), channel_id=1, source_target_pairs={{0,1},{1,2},{2,3},{3,0},{4,5},{5,6},{6,7},{7,4},{8,9},{9,10},{10,1... | collective-permute-start | bytes 3538952 | tf_op jit(solution)/shard_map/ppermute | solution.py:22
  269.0 14.0 %copy-start.16 = (bf16[576,1536]{1,0:T(8,128)(2,1)S(1)}, bf16[576,1536]{1,0:T(8,128)(2,1)}, u32[]{:S(2)}) copy-start(bf16[576,1536]{1,0:T(8,128)(2,1)} %param.7) | copy-start | bytes 5308420
  269.1 14.0 %copy-start.17 = (f32[1536]{0:T(1024)S(1)}, f32[1536]{0:T(1024)}, u32[]{:S(2)}) copy-start(f32[1536]{0:T(1024)} %param.12) | copy-start | bytes 18436
  283.0 11.5 %copy-start.1 = (s32[32,3]{0,1:T(4,128)S(1)}, s32[32,3]{0,1:T(4,128)}, u32[]{:S(2)}) copy-start(s32[32,3]{0,1:T(4,128)} %param.13) | copy-start | bytes 1156
  (3 other events, 3.5 us)
